TPU v7x, 256 devices: a whole 4x4x8 slice. The times are simulated.
256 devices in a mesh: region: 32 (over z, y), angle: 8 (over x, core).
Axes of the slice: x: 4, y: 4, z: 8, core: 2. Of those that a mesh axis runs over, the one named last changes fastest.
Arguments:
- volume: float32 [512, 128, 128], P('region'), may hold values from -6 to 6
- blocks: bfloat16 [65536, 128, 128], P(('region', 'angle')), may hold values from -0.1875 to 0.1875
- tile_of: int32 [65536], P(('region', 'angle')), may hold values from 0 to 15
- slot_of: int32 [65536], P(('region', 'angle')), may hold values from 0 to 31
- live_count: int32 [256], P(('region', 'angle')), may hold values from 96 to 256, as said below
- ray_of: int32 [8192], P(('region', 'angle')), may hold values from 0 to 7
- sinogram: float32 [2048, 128, 128], P(('region', 'angle')), may hold values from -6 to 6
- ray_weight: float32 [2048, 128], P(('region', 'angle')), may hold values from 0.5 to 2
- pixel_weight: float32 [512, 128], P('region'), may hold values from 0.1 to 0.5
Outputs:
- updated: float32 [512, 128, 128], P(('region', 'angle'))
- residual: float32 [2048, 128, 128], P(('region', 'angle'))
Inputs may be any that keep to these rules, and one draw needn't show every extreme that they name: Blocks at positions 256 * d + j with j < live_count[d] are in use, the others are ignored; every device uses at least 96 blocks, and some device uses all 256.
All inputs are finite; a program needn't handle non-finite values.
Results may differ from a plain program's by a relative error of at most 0.0039.
Values may be sent and summed in bfloat16 or wider, within the bound.
A program may use at most 128 MiB of HBM per device.

v0:
```python
import jax
import jax.numpy as jnp
from jax import lax
from jax.sharding import PartitionSpec as P


def body(volume, blocks, tile_of, slot_of, live_count, ray_of, sinogram, ray_weight, pixel_weight):
    n_region = lax.axis_size("region")
    n_angle = lax.axis_size("angle")
    slot_count = ray_of.shape[0]
    capacity = slot_count // n_region
    ray_rows = sinogram.shape[0]
    tile_rows = volume.shape[0]
    entries = blocks.shape[0]
    is_live = jnp.arange(entries, dtype=jnp.int32) < live_count[0]
    volume_b = volume.astype(jnp.bfloat16)
    picked = volume_b[tile_of]
    forward = jnp.einsum("esp,erp->esr", picked, blocks, preferred_element_type=jnp.float32)
    slot_ids = jnp.where(is_live, slot_of, slot_count)
    partial_value = jax.ops.segment_sum(forward, slot_ids, num_segments=slot_count + 1)[:slot_count]
    owner_maps = lax.all_to_all(
        ray_of.reshape(n_region, capacity), "region", split_axis=0, concat_axis=0, tiled=True
    )
    ray_target = (jnp.arange(n_region, dtype=jnp.int32)[:, None] * ray_rows + owner_maps).reshape(
        slot_count
    )
    dense_sums = jax.ops.segment_sum(partial_value, ray_target, num_segments=n_region * ray_rows)
    projection = lax.psum_scatter(dense_sums, "region", scatter_dimension=0, tiled=True)
    residual = ray_weight[:, None, :] * (sinogram - projection)
    residual_b = residual.astype(jnp.bfloat16)
    gathered = lax.all_gather(residual_b, "region", axis=0, tiled=True)
    returned = gathered[ray_target]
    slot_rows = returned[slot_of]
    backward = jnp.einsum("esr,erp->esp", slot_rows, blocks, preferred_element_type=jnp.float32)
    tile_ids = jnp.where(is_live, tile_of, tile_rows)
    gradient = jax.ops.segment_sum(backward, tile_ids, num_segments=tile_rows + 1)[:tile_rows]
    per_angle = tile_rows // n_angle
    first_tile = lax.axis_index("angle") * per_angle
    all_tiles = lax.psum(gradient, "angle")
    my_share = lax.dynamic_slice_in_dim(all_tiles, first_tile, per_angle, 0)
    volume_part = lax.dynamic_slice_in_dim(volume, first_tile, per_angle, 0)
    weight_part = lax.dynamic_slice_in_dim(pixel_weight, first_tile, per_angle, 0)
    updated = volume_part + weight_part[:, None, :] * my_share
    return (updated, residual)


def solution(mesh):
    placed = (
        P("region", None, None),
        P(("region", "angle"), None, None),
        P(("region", "angle")),
        P(("region", "angle")),
        P(("region", "angle")),
        P(("region", "angle")),
        P(("region", "angle"), None, None),
        P(("region", "angle"), None),
        P("region", None),
    )
    return jax.shard_map(
        body,
        mesh=mesh,
        in_specs=placed,
        out_specs=(P(("region", "angle"), None, None), P(("region", "angle"), None, None)),
        check_vma=False,
    )
```

profile of v0, /device:TPU:1, one launch (start us, length us, event | category | flops | bytes accessed | tf_op | source)
XLA Modules:
  0.0 579.4 jit_solution(5974382091438254306)
XLA Ops:
  7.2 0.0 copy-start
  7.2 1.3 copy.12
  8.5 12.0 %all-to-all-start = ((s32[32,1,1]{2,1,0:T(1,128)}), s32[32,1,1]{2,1,0:T(1,128)S(1)}, u32[]{:S(2)}, u32[]{:S(2)}) async-start(s32[32,1,1]{2,1,0:T(1,128)} %copy.12), calls=%async_computation | async-start | bytes 32768 | tf_op jit(solution)/shard_map/all_to_all | solution.py:21
  20.6 0.0 reduce-scatter.2.cloned.1.call-start
  21.3 0.7 compare_select_fusion
  22.0 1.3 convert_element_type.6
  23.3 8.6 %gather_fusion = bf16[256,128,128]{2,1,0:T(8,128)(2,1)} fusion(bf16[16,128,128]{2,1,0:T(8,128)(2,1)S(1)} %convert_element_type.6, s32[1024]{0:T(1024)S(1)} %pad_clamp_fusion.2), kind=kCustom, calls=%fused_computation | custom fusion | bytes 16778240 | tf_op jit(solution)/shard_map/gather | solution.py:17
  31.9 17.4 %fusion.5 = f32[256,128,128]{2,1,0:T(8,128)} fusion(bf16[256,128,128]{2,1,0:T(8,128)(2,1)} %gather_fusion, bf16[256,128,128]{2,1,0:T(8,128)(2,1)} %param.10), kind=kOutput, calls=%fused_computation.22 | convolution fusion | flops 1073741824 | bytes 33554432 | tf_op jit(solution)/shard_map/esp,erp->esr/dot_general | solution.py:18
  49.3 0.2 broadcast_in_dim.36
  49.5 33.2 %scatter_fusion = f32[33,128,128]{2,1,0:T(8,128)S(1)} fusion(f32[33,128,128]{2,1,0:T(8,128)S(1)} %broadcast_in_dim.36, s32[256]{0:T(256)S(1)} %get-tuple-element.5, f32[256,128,128]{2,1,0:T(8,128)} %fusion.5), kind=kCustom, calls=%fused_computation.3 | custom fusion | flops 4194304 | bytes 50332672 | tf_op jit(solution)/shard_map/scatter-add | solution.py:20
  82.7 1.5 slice.14
  84.2 0.0 all-to-all-done
  84.2 0.7 reduce
  84.8 0.0 copy-start.1
  84.9 7.8 %broadcast_in_dim.35 = f32[256,128,128]{2,1,0:T(8,128)} broadcast(f32[]{:T(128)} %constant.12.clone.1), dimensions={} | broadcast | bytes 16777220 | tf_op jit(solution)/shard_map/broadcast_in_dim | solution.py:27
  92.7 0.0 copy-done.1
  92.7 6.3 %scatter_fusion.1 = f32[256,128,128]{2,1,0:T(8,128)} fusion(f32[256,128,128]{2,1,0:T(8,128)} %broadcast_in_dim.35, s32[32]{0:T(128)S(1)} %get-tuple-element.9, f32[32,128,128]{2,1,0:T(8,128)S(1)} %copy-done.1), kind=kCustom, calls=%fused_computation.4 | custom fusion | flops 524288 | bytes 6291584 | tf_op jit(solution)/shard_map/scatter-add | solution.py:27
  99.0 0.0 copy-start.2
  99.0 0.0 copy-start.3
  99.0 0.0 reduce-scatter.2.cloned.1.call-update
  99.0 0.0 all-gather.2.cloned.1.call-start
  99.0 244.9 %reduce-scatter.2.cloned.1.call-done = f32[8,128,128]{2,1,0:T(8,128)} async-done(((f32[256,128,128]{2,1,0:T(8,128)}), f32[8,128,128]{2,1,0:T(8,128)}) %reduce-scatter.2.cloned.1.call-update) | async-done | bytes 524304 | tf_op jit(solution)/shard_map/reduce_scatter | solution.py:28
  344.0 0.0 copy-done.2
  344.0 0.0 copy-done.3
  344.0 2.1 fusion.4
  346.1 0.0 all-gather.2.cloned.1.call-update
  346.1 0.2 all-reduce.2.cloned.1.call-start
  346.4 100.3 %all-gather.2.cloned.1.call-done = bf16[256,128,128]{2,1,0:T(8,128)(2,1)} async-done(((bf16[8,128,128]{2,1,0:T(8,128)(2,1)}), bf16[256,128,128]{2,1,0:T(8,128)(2,1)}) %all-gather.2.cloned.1.call-update) | async-done | bytes 8388624 | tf_op jit(solution)/shard_map/all_gather | solution.py:31
  446.7 4.1 gather_fusion.1
  450.8 8.6 %gather_fusion.2 = bf16[256,128,128]{2,1,0:T(8,128)(2,1)} fusion(bf16[32,128,128]{2,1,0:T(8,128)(2,1)S(1)} %gather_fusion.1, s32[1024]{0:T(1024)S(1)} %pad_clamp_fusion), kind=kCustom, calls=%fused_computation.2 | custom fusion | bytes 16778240 | tf_op jit(solution)/shard_map/gather | solution.py:33
  459.4 13.8 %fusion.6 = f32[256,128,128]{2,1,0:T(8,128)} fusion(bf16[256,128,128]{2,1,0:T(8,128)(2,1)} %gather_fusion.2, bf16[256,128,128]{2,1,0:T(8,128)(2,1)} %param.10), kind=kOutput, calls=%fused_computation.23 | convolution fusion | flops 1073741824 | bytes 33554432 | tf_op jit(solution)/shard_map/esr,erp->esp/dot_general | solution.py:34
  473.2 0.1 broadcast_in_dim.32
  473.4 33.2 %scatter_fusion.2 = f32[17,128,128]{2,1,0:T(8,128)S(1)} fusion(f32[17,128,128]{2,1,0:T(8,128)S(1)} %broadcast_in_dim.32, s32[256]{0:T(256)S(1)} %get-tuple-element.10, f32[256,128,128]{2,1,0:T(8,128)} %fusion.6), kind=kCustom, calls=%fused_computation.5 | custom fusion | flops 4194304 | bytes 50332672 | tf_op jit(solution)/shard_map/scatter-add | solution.py:36
  506.5 1.1 slice.15
  507.6 0.0 all-reduce.2.cloned.1.call-update
  507.6 0.0 copy-done
  507.7 63.6 %all-reduce.2.cloned.1.call-done = f32[16,128,128]{2,1,0:T(8,128)} async-done(((f32[16,128,128]{2,1,0:T(8,128)}), f32[16,128,128]{2,1,0:T(8,128)}) %all-reduce.2.cloned.1.call-update) | async-done | bytes 1048592 | tf_op jit(solution)/shard_map/psum | solution.py:39
  571.3 1.6 multiply_add_fusion
  (5 shorter events, 0.0 us)
Async XLA Ops:
  7.2 500.5 %copy-start = (f32[16,128]{1,0:T(8,128)S(1)}, f32[16,128]{1,0:T(8,128)}, u32[]{:S(2)}) copy-start(f32[16,128]{1,0:T(8,128)} %param.17) | copy-start | bytes 24580
  8.5 75.6 %all-to-all-start = ((s32[32,1,1]{2,1,0:T(1,128)}), s32[32,1,1]{2,1,0:T(1,128)S(1)}, u32[]{:S(2)}, u32[]{:S(2)}) async-start(s32[32,1,1]{2,1,0:T(1,128)} %copy.12), calls=%async_computation | async-start | bytes 32768 | tf_op jit(solution)/shard_map/all_to_all | solution.py:21
  20.6 323.4 %reduce-scatter.2.cloned.1.call-start = ((), (), s32[]{:S(2)}) async-start(), calls=%async_computation.2 | async-start | bytes 17301504 | tf_op jit(solution)/shard_map/reduce_scatter | solution.py:28
  84.8 7.9 %copy-start.1 = (f32[32,128,128]{2,1,0:T(8,128)S(1)}, f32[32,128,128]{2,1,0:T(8,128)}, u32[]{:S(2)}) copy-start(f32[32,128,128]{2,1,0:T(8,128)} %slice.14) | copy-start | bytes 6291460
  99.0 245.0 %copy-start.2 = (f32[8,128,128]{2,1,0:T(8,128)S(1)}, f32[8,128,128]{2,1,0:T(8,128)}, u32[]{:S(2)}) copy-start(f32[8,128,128]{2,1,0:T(8,128)} %param.15) | copy-start | bytes 1572868
  99.0 245.0 %copy-start.3 = (f32[8,128]{1,0:T(8,128)S(1)}, f32[8,128]{1,0:T(8,128)}, u32[]{:S(2)}) copy-start(f32[8,128]{1,0:T(8,128)} %param.16) | copy-start | bytes 12292
  99.0 347.7 %all-gather.2.cloned.1.call-start = ((), (), s32[]{:S(2)}) async-start(), calls=%async_computation.3 | async-start | bytes 8650752 | tf_op jit(solution)/shard_map/all_gather | solution.py:31
  346.1 225.1 %all-reduce.2.cloned.1.call-start = ((), (), s32[]{:S(2)}) async-start(), calls=%async_computation.4 | async-start | bytes 2097152 | tf_op jit(solution)/shard_map/psum | solution.py:39
Sparse Core Ops, SparseCore 0:
  99.1 244.8 reduce-scatter.1
  346.6 100.0 all-gather.1
  507.8 63.4 all-reduce.1
where the time goes:
time: 582 us; the launch traced here: 579 us
  waiting for transfers between devices  409 us (70%)
  other arithmetic  79 us (14%)
  local copies, waits for them, and re-layouts  33.5 us (6%)
  matrix products  31.2 us (5%)
  between operations  14.5 us (2%)
  starting transfers between devices  12.3 us (2%)
    reduce_scatter x1, waiting for transfers between devices, body(): lax.psum_scatter(dense_sums, 'region', scatter_dimension=0, tiled=True)  245 us
    all_gather x1, waiting for transfers between devices, body(): gathered = lax.all_gather(residual_b, 'region', axis=0, tiled=True)  100 us
    psum x1, waiting for transfers between devices, body(): all_tiles = lax.psum(gradient, 'angle')  63.6 us
    scatter-add x1, other arithmetic, body(): jax.ops.segment_sum(forward, slot_ids, num_segments=slot_count + 1)  33.2 us
    scatter-add x1, other arithmetic, body(): jax.ops.segment_sum(backward, tile_ids, num_segments=tile_rows + 1)  33.2 us
    dot_general x1, matrix products, body(): jnp.einsum('esp,erp->esr', picked, blocks, preferred_element_type=jnp.flo...  17.4 us
    dot_general x1, matrix products, body(): jnp.einsum('esr,erp->esp', slot_rows, blocks, preferred_element_type=jnp....  13.8 us
    all_to_all x1, starting transfers between devices, body(): lax.all_to_all(ray_of.reshape(n_region, capacity), 'region', split_axis=0...  12 us
  transfers between devices with their start and end apart: 4, of which 3 were waited for; matrix products, arithmetic and copies ran while one was open for 11% of the time, Pallas kernels for 0%

commit v1 on v0

v1 whole, which is shorter than its diff:
```python
import functools

import jax
import jax.numpy as jnp
from jax import lax
from jax.experimental import pallas as pl
from jax.experimental.pallas import tpu as pltpu
from jax.sharding import PartitionSpec as P

MESH = pl.DeviceIdType.MESH
BF = jnp.bfloat16
F32 = jnp.float32
I32 = jnp.int32

CHUNKS = 2
UNROLL = 8
NY = 4


def iota(shape, dim):
    return lax.broadcasted_iota(I32, shape, dim)


def order(key_row, live_row, payload_row, pad, keys, group, places):
    n = key_row.shape[1]
    row, col = iota((n, n), 0), iota((n, n), 1)
    key_row = jnp.where(live_row, key_row, keys)
    diag = row == col
    key_col = jnp.sum(jnp.where(diag, key_row, 0), axis=1, keepdims=True)
    payload_col = jnp.sum(jnp.where(diag, payload_row, 0), axis=1, keepdims=True)
    earlier = jnp.where((key_col == key_row) & (col < row), 1, 0)
    rank_col = jnp.sum(earlier, axis=1, keepdims=True)
    lane = iota((n, 128), 1)
    same = key_col == lane
    count_row = jnp.sum(jnp.where(same, 1, 0), axis=0, keepdims=True)
    run_row = (count_row + (group - 1)) & -group
    start_col = jnp.sum(jnp.where(lane < key_col, run_row, 0), axis=1, keepdims=True)
    place_col = jnp.where(key_col < keys, start_col + rank_col, 1 << 20)
    hit = place_col == iota((n, places), 1)
    entry = iota((n, places), 0)
    src = jnp.sum(jnp.where(hit, entry, 0), axis=0, keepdims=True)
    payload = jnp.sum(jnp.where(hit, payload_col - pad, 0), axis=0, keepdims=True) + pad
    opens = jnp.sum(jnp.where(hit & (rank_col == 0), 1, 0), axis=0, keepdims=True)
    last = jnp.max(jnp.where(same, place_col, -1), axis=0, keepdims=True)
    return src, payload, opens, last


def kernel(
    n_region, n_angle, chunks,
    count_s, ray_s, tile_v, slot_v, ray_v, rw_v, pw_v, volume_h, blocks_h, sino_h,
    updated_h, residual_h,
    blocks, vol, sino, vol_b, runs_f, runs_b, runs_p, rows_v, rows_s,
    send1, recv1, res, res_b, send2, recv2, grad, send3, recv3, upd,
    sem_in, sem_rows, sem_out, ssem1, rsem1, ssem2, rsem2, ssem3, rsem3,
):
    r = lax.axis_index("region")
    a = lax.axis_index("angle")
    z, y = r // NY, lax.rem(r, NY)
    nz = n_region // NY
    entries = blocks.shape[0]
    tiles = vol.shape[0]
    slots = n_region
    rays = sino.shape[0]
    size = vol.shape[1]
    m = size // chunks
    pairs_f = runs_f.shape[0] - 1
    pairs_b = runs_b.shape[0] - 1
    share = tiles // n_angle

    load_b = pltpu.make_async_copy(blocks_h, blocks, sem_in.at[0])
    load_v = pltpu.make_async_copy(volume_h, vol, sem_in.at[1])
    load_s = pltpu.make_async_copy(sino_h, sino, sem_in.at[2])
    load_v.start()
    load_b.start()
    load_s.start()

    far = lambda d, n: min(d, n - d)
    steps = [(dz, dy) for dz in range(nz) for dy in range(NY) if (dz, dy) != (0, 0)]
    steps.sort(key=lambda o: -(far(o[0], nz) + far(o[1], NY)))
    peers = [lax.rem(z + dz, nz) * NY + lax.rem(y + dy, NY) for dz, dy in steps]
    others = [lax.rem(a + k, n_angle) for k in range(1, n_angle)]
    barrier = pltpu.get_barrier_semaphore()
    for peer in peers:
        pl.semaphore_signal(barrier, inc=1, device_id=(peer, a), device_id_type=MESH)
    for other in others:
        pl.semaphore_signal(barrier, inc=1, device_id=(r, other), device_id_type=MESH)

    live = lax.broadcasted_iota(I32, (1, entries), 1) < count_s[0]
    tile_row, slot_row, ray_row = tile_v[...], slot_v[...], ray_v[...]
    places = rows_v.shape[1]
    every = lax.broadcasted_iota(I32, ray_row.shape, 1) < n_region
    empty = lambda last, group, none: jnp.where(last < 0, none, last >> (group - 1))
    pad = lambda x: jnp.concatenate([x, jnp.zeros((1, places - x.shape[1]), I32)], axis=1)
    src, payload, opens, last = order(slot_row, live, tile_row, tiles, slots, 2, places)
    rows = [src, payload, opens, pad(empty(last, 2, pairs_f))]
    src, payload, opens, last = order(tile_row, live, slot_row, slots, tiles, 2, places)
    rows += [src, payload, opens, pad(empty(last, 2, pairs_b))]
    src, _, opens, last = order(ray_row, every, ray_row, 0, rays, 1, 128)
    rows += [pad(src), pad(opens), pad(empty(last, 1, n_region))]
    for i, row in enumerate(rows):
        rows_v[i : i + 1, :] = row
    to_scalar = pltpu.make_async_copy(rows_v, rows_s, sem_rows)
    to_scalar.start()

    load_v.wait()
    for t in range(tiles):
        vol_b[t] = vol[t].astype(BF)
    vol_b[tiles] = jnp.zeros((size, size), BF)
    for c in range(chunks):
        recv2[c][slots] = jnp.zeros((m, size), BF)
    runs_f[pairs_f] = jnp.zeros((m, size), BF)
    runs_b[pairs_b] = jnp.zeros((m, size), F32)
    runs_p[n_region] = jnp.zeros((m, size), F32)
    to_scalar.wait()
    load_b.wait()

    def products(left, base, transposed, runs, pairs):
        def step(g, total):
            for u in range(UNROLL):
                p = g * UNROLL + u
                e0, e1 = rows_s[base, 2 * p], rows_s[base, 2 * p + 1]
                k0, k1 = rows_s[base + 1, 2 * p], rows_s[base + 1, 2 * p + 1]
                opened = rows_s[base + 2, 2 * p]
                lhs = jnp.concatenate([left[k0], left[k1]], axis=1)
                rhs = jnp.concatenate([blocks[e0], blocks[e1]], axis=1 if transposed else 0)
                dims = (((1,), (1,)), ((), ())) if transposed else (((1,), (0,)), ((), ()))
                product = lax.dot_general(lhs, rhs, dims, preferred_element_type=F32)
                total = jnp.where(opened > 0, 0.0, total) + product
                runs[p] = total.astype(runs.dtype)
            return total

        lax.fori_loop(0, pairs // UNROLL, step, jnp.zeros((m, size), F32))

    def exchange(src, dst, ssem, rsem, c):
        rows_at = pl.ds(c * m, m)
        for peer in peers:
            pltpu.make_async_remote_copy(
                src_ref=src.at[peer, rows_at], dst_ref=dst[c].at[r],
                send_sem=ssem.at[c], recv_sem=rsem.at[c], device_id=(peer, a), device_id_type=MESH,
            ).start()
        dst[c][r] = src[r, rows_at, :]

    def arrived(dst, sem, c):
        part = dst[c].at[pl.ds(0, n_region - 1)]
        pltpu.make_async_copy(part, part, sem.at[c]).wait()

    for c in range(chunks):
        rows_at = pl.ds(c * m, m)
        products(vol_b.at[:, rows_at], 0, True, runs_f, pairs_f)
        for s in range(slots):
            send1[s, rows_at, :] = runs_f[rows_s[3, s]]
        if c == 0:
            pl.semaphore_wait(barrier, len(peers) + len(others))
        exchange(send1, recv1, ssem1, rsem1, c)

    load_s.wait()
    for c in range(chunks):
        rows_at = pl.ds(c * m, m)
        arrived(recv1, rsem1, c)
        total = jnp.zeros((m, size), F32)
        for k in range(n_region):
            total = jnp.where(rows_s[9, k] > 0, 0.0, total) + recv1[c][rows_s[8, k]].astype(F32)
            runs_p[k] = total
        for j in range(rays):
            value = rw_v[j : j + 1, :] * (sino[j, rows_at, :] - runs_p[rows_s[10, j]])
            res[j, rows_at, :] = value
            res_b[j, rows_at, :] = value.astype(BF)
        for s in range(n_region):
            send2[s, rows_at, :] = res_b[ray_s[s], rows_at, :]
        exchange(send2, recv2, ssem2, rsem2, c)
    out_r = pltpu.make_async_copy(res, residual_h, sem_out.at[0])
    out_r.start()

    for c in range(chunks):
        rows_at = pl.ds(c * m, m)
        arrived(recv2, rsem2, c)
        products(recv2[c], 4, False, runs_b, pairs_b)
        for t in range(tiles):
            value = runs_b[rows_s[7, t]]
            grad[t, rows_at, :] = value
            send3[t // share, c, t % share] = value.astype(BF)
        for other in others:
            pltpu.make_async_remote_copy(
                src_ref=send3.at[other, c], dst_ref=recv3.at[a, c],
                send_sem=ssem3.at[c], recv_sem=rsem3.at[c], device_id=(r, other), device_id_type=MESH,
            ).start()
        recv3[a, c] = jnp.zeros((share, m, size), BF)

    for c in range(chunks):
        rows_at = pl.ds(c * m, m)
        part = recv3.at[pl.ds(0, n_angle - 1), c]
        pltpu.make_async_copy(part, part, rsem3.at[c]).wait()
        for t in range(share):
            mine = a * share + t
            total = grad[mine, rows_at, :]
            for k in range(n_angle):
                total = total + recv3[k, c, t].astype(F32)
            upd[t, rows_at, :] = vol[mine, rows_at, :] + pw_v[pl.ds(mine, 1), :] * total
    out_u = pltpu.make_async_copy(upd, updated_h, sem_out.at[1])
    out_u.start()

    for c in range(chunks):
        for src, sem in ((send1, ssem1), (send2, ssem2)):
            part = src.at[pl.ds(0, n_region - 1), pl.ds(c * m, m)]
            pltpu.make_async_copy(part, part, sem.at[c]).wait()
        part = send3.at[pl.ds(0, n_angle - 1), c]
        pltpu.make_async_copy(part, part, ssem3.at[c]).wait()
    out_r.wait()
    out_u.wait()


def up(value, step):
    return -(-value // step) * step


def body(volume, blocks, tile_of, slot_of, live_count, ray_of, sinogram, ray_weight, pixel_weight):
    n_region = lax.axis_size("region")
    n_angle = lax.axis_size("angle")
    entries, size, _ = blocks.shape
    tiles, rays = volume.shape[0], sinogram.shape[0]
    chunks = CHUNKS
    m = size // chunks
    share = tiles // n_angle
    pairs_f = up((entries + n_region) // 2, UNROLL)
    pairs_b = up((entries + tiles) // 2, UNROLL)
    places = up(2 * max(pairs_f, pairs_b), 128)
    ray_row = jnp.pad(ray_of, (0, 128 - n_region)).reshape(1, 128)
    smem = pl.BlockSpec(memory_space=pltpu.SMEM)
    vmem = pl.BlockSpec(memory_space=pltpu.VMEM)
    hbm = pl.BlockSpec(memory_space=pl.ANY)
    return pl.pallas_call(
        functools.partial(kernel, n_region, n_angle, chunks),
        out_shape=(
            jax.ShapeDtypeStruct((share, size, size), F32),
            jax.ShapeDtypeStruct((rays, size, size), F32),
        ),
        in_specs=[smem, smem, vmem, vmem, vmem, vmem, vmem, hbm, hbm, hbm],
        out_specs=(hbm, hbm),
        scratch_shapes=[
            pltpu.VMEM((entries, size, size), BF),
            pltpu.VMEM((tiles, size, size), F32),
            pltpu.VMEM((rays, size, size), F32),
            pltpu.VMEM((tiles + 1, size, size), BF),
            pltpu.VMEM((pairs_f + 1, m, size), BF),
            pltpu.VMEM((pairs_b + 1, m, size), F32),
            pltpu.VMEM((n_region + 1, m, size), F32),
            pltpu.VMEM((16, places), I32),
            pltpu.SMEM((16, places), I32),
            pltpu.VMEM((n_region, size, size), BF),
            [pltpu.VMEM((n_region, m, size), BF)] * chunks,
            pltpu.VMEM((rays, size, size), F32),
            pltpu.VMEM((rays, size, size), BF),
            pltpu.VMEM((n_region, size, size), BF),
            [pltpu.VMEM((n_region + 1, m, size), BF)] * chunks,
            pltpu.VMEM((tiles, size, size), F32),
            pltpu.VMEM((n_angle, chunks, share, m, size), BF),
            pltpu.VMEM((n_angle, chunks, share, m, size), BF),
            pltpu.VMEM((share, size, size), F32),
            pltpu.SemaphoreType.DMA((3,)),
            pltpu.SemaphoreType.DMA,
            pltpu.SemaphoreType.DMA((2,)),
        ]
        + [pltpu.SemaphoreType.DMA((chunks,))] * 6,
        compiler_params=pltpu.CompilerParams(
            collective_id=0, has_side_effects=True, vmem_limit_bytes=56 * 2**20
        ),
    )(
        live_count, ray_of, tile_of.reshape(1, entries), slot_of.reshape(1, entries), ray_row,
        ray_weight, pixel_weight, volume, blocks, sinogram,
    )


def solution(mesh):
    placed = (
        P("region", None, None),
        P(("region", "angle"), None, None),
        P(("region", "angle")),
        P(("region", "angle")),
        P(("region", "angle")),
        P(("region", "angle")),
        P(("region", "angle"), None, None),
        P(("region", "angle"), None),
        P("region", None),
    )
    return jax.shard_map(
        body,
        mesh=mesh,
        in_specs=placed,
        out_specs=(P(("region", "angle"), None, None), P(("region", "angle"), None, None)),
        check_vma=False,
    )
```

time: 582 us -> 81.1 us (0.14)
  waiting for transfers between devices: 409 us -> 0 us
  other arithmetic: 79 us -> 0 us
  Pallas kernels: 0 us -> 75 us
  matrix products: 31.2 us -> 0 us
  local copies, waits for them, and re-layouts: 33.5 us -> 4.61 us
  between operations: 14.5 us -> 1.29 us
  starting transfers between devices: 12.3 us -> 0 us
    reduce_scatter x1 -> x0, waiting for transfers between devices: 245 us -> none  [body(): lax.psum_scatter(dense_sums, 'region', scatter_dimension=0, tiled=True)]
    all_gather x1 -> x0, waiting for transfers between devices: 100 us -> none  [body(): gathered = lax.all_gather(residual_b, 'region', axis=0, tiled=True)]
    pallas_call x0 -> x1, Pallas kernels: none -> 75 us  [body(): pl.pallas_call(functools.partial(kernel, n_region, n_angle, chunks), out_...]
    scatter-add x3 -> x0, other arithmetic: 72.6 us -> none  [the longest x1 33.2 us: body(): jax.ops.segment_sum(forward, slot_ids, num_segments=slot_count + 1)]
    psum x1 -> x0, waiting for transfers between devices: 63.6 us -> none  [body(): all_tiles = lax.psum(gradient, 'angle')]
    dot_general x2 -> x0, matrix products: 31.2 us -> none  [the longest x1 17.4 us: body(): jnp.einsum('esp,erp->esr', picked, blocks, preferred_element_type=jnp.flo...]
    gather x3 -> x0, local copies, waits for them, and re-layouts: 21.3 us -> none  [the longest x1 8.6 us: body(): slot_rows = returned[slot_of]]
    all_to_all x1 -> x0, starting transfers between devices: 12 us -> none  [body(): lax.all_to_all(ray_of.reshape(n_region, capacity), 'region', split_axis=0...]
  transfers between devices with their start and end apart: 4 -> 0, of which waited for: 3 -> 0; matrix products, arithmetic and copies ran while one was open for 11% -> 0% of each run, Pallas kernels for 0% -> 0%
where the time goes in v1:
time: 81.1 us; the launch traced here: 80.9 us
  Pallas kernels  75 us (92%)
  local copies, waits for them, and re-layouts  4.61 us (6%)
  between operations  1.29 us (2%)
    pallas_call x1, Pallas kernels, body(): pl.pallas_call(functools.partial(kernel, n_region, n_angle, chunks), out_...  75 us
    unnamed x2, local copies, waits for them, and re-layouts  3.44 us

profile of v1, /device:TPU:1, one launch (start us, length us, event | category | flops | bytes accessed | tf_op | source)
XLA Modules:
  0.0 80.9 jit_solution(139745894988672054)
XLA Ops:
  1.3 1.2 %pad_bitcast_fusion.ray_v = s32[1,128]{1,0:T(1,128)} fusion(s32[32]{0:T(128)} %ray_s.1), kind=kLoop, calls=%fused_computation | loop fusion | bytes 640 | tf_op jit(solution)/shard_map/reshape | solution.py:227
  2.4 75.0 %shard_map.104 = (f32[2,128,128]{2,1,0:T(8,128)}, f32[8,128,128]{2,1,0:T(8,128)}) custom-call(s32[1]{0:T(128)S(6)} %copy.13.count_s, s32[32]{0:T(128)} %ray_s.1, s32[1,256]{1,0:T(1,128)} %bitcast.4, s32[1,256]{1,0:T(1,128)} %bitcast.5, s32[1,128]{1,0:T(1,128)} %pad_bitcast_fusion.ray_v, f32[8,128]{1,0:T(8,128)} %rw_v.1, f32[16,128]{1,0:T(8,128)} %pw_v.1, ...), custom_call_target="tpu_custom_call" | custom-call | tf_op jit(solution)/shard_map/pallas_call | solution.py:231
  77.5 1.6 %copy.14 = f32[2,128,128]{2,1,0:T(8,128)} copy(f32[2,128,128]{2,1,0:T(8,128)} %get-tuple-element.4) | data formatting | bytes 262144
  79.0 1.9 %copy.15 = f32[8,128,128]{2,1,0:T(8,128)} copy(f32[8,128,128]{2,1,0:T(8,128)} %get-tuple-element.5) | data formatting | bytes 1048576

commit v2 on v1

v2 whole, which is shorter than its diff:
```python
import functools

import jax
import jax.numpy as jnp
from jax import lax
from jax.experimental import pallas as pl
from jax.experimental.pallas import tpu as pltpu
from jax.sharding import PartitionSpec as P

MESH = pl.DeviceIdType.MESH
BF = jnp.bfloat16
F32 = jnp.float32
I32 = jnp.int32

SIZES = (48, 48, 32)
UNROLL_F, UNROLL_B = 18, 17
LOADS = 4
NY = 4


def iota(shape, dim):
    return lax.broadcasted_iota(I32, shape, dim)


def order(key_row, live_row, payload_row, pad, keys, group, places):
    n = key_row.shape[1]
    row, col = iota((n, n), 0), iota((n, n), 1)
    key_row = jnp.where(live_row, key_row, keys)
    diag = row == col
    key_col = jnp.sum(jnp.where(diag, key_row, 0), axis=1, keepdims=True)
    payload_col = jnp.sum(jnp.where(diag, payload_row, 0), axis=1, keepdims=True)
    earlier = jnp.where((key_col == key_row) & (col < row), 1, 0)
    rank_col = jnp.sum(earlier, axis=1, keepdims=True)
    lane = iota((n, 128), 1)
    same = key_col == lane
    count_row = jnp.sum(jnp.where(same, 1, 0), axis=0, keepdims=True)
    run_row = (count_row + (group - 1)) & -group
    start_col = jnp.sum(jnp.where(lane < key_col, run_row, 0), axis=1, keepdims=True)
    place_col = jnp.where(key_col < keys, start_col + rank_col, 1 << 20)
    hit = place_col == iota((n, places), 1)
    entry = iota((n, places), 0)
    src = jnp.sum(jnp.where(hit, entry, 0), axis=0, keepdims=True)
    payload = jnp.sum(jnp.where(hit, payload_col - pad, 0), axis=0, keepdims=True) + pad
    opens = jnp.sum(jnp.where(hit & (rank_col == 0), 1, 0), axis=0, keepdims=True)
    last = jnp.max(jnp.where(same, place_col, -1), axis=0, keepdims=True)
    return src, payload, opens, last


def kernel(
    n_region, n_angle, sizes,
    count_s, ray_s, tile_v, slot_v, ray_v, rw_v, pw_v, volume_h, blocks_h, sino_h,
    upd, res,
    blocks, vol, sino, vol_b, runs_f, runs_b, runs_p, rows_v, rows_s,
    send1, recv1, res_b, send2, recv2, grad, send3, recv3,
    sem_in, sem_rows, ssem1, rsem1, ssem2, rsem2, ssem3, rsem3,
):
    r = lax.axis_index("region")
    a = lax.axis_index("angle")
    z, y = r // NY, lax.rem(r, NY)
    nz = n_region // NY
    entries = blocks.shape[0]
    tiles = vol.shape[0]
    slots = n_region
    rays = sino.shape[0]
    size = vol.shape[1]
    chunks = len(sizes)
    parts = [pl.ds(sum(sizes[:c]), m) for c, m in enumerate(sizes)]
    most = max(sizes)
    pairs_f = runs_f.shape[0] - 1
    pairs_b = runs_b.shape[0] - 1
    share = tiles // n_angle

    piece = entries // LOADS
    load_b = [
        pltpu.make_async_copy(blocks_h.at[pl.ds(i * piece, piece)], blocks.at[pl.ds(i * piece, piece)], sem_in.at[2 + i])
        for i in range(LOADS)
    ]
    load_v = pltpu.make_async_copy(volume_h, vol, sem_in.at[0])
    load_s = pltpu.make_async_copy(sino_h, sino, sem_in.at[1])
    load_v.start()
    for load in load_b:
        load.start()
    load_s.start()

    far = lambda d, n: min(d, n - d)
    steps = [(dz, dy) for dz in range(nz) for dy in range(NY) if (dz, dy) != (0, 0)]
    steps.sort(key=lambda o: -(far(o[0], nz) + far(o[1], NY)))
    peers = [lax.rem(z + dz, nz) * NY + lax.rem(y + dy, NY) for dz, dy in steps]
    others = [lax.rem(a + k, n_angle) for k in range(1, n_angle)]
    barrier = pltpu.get_barrier_semaphore()
    for peer in peers:
        pl.semaphore_signal(barrier, inc=1, device_id=(peer, a), device_id_type=MESH)
    for other in others:
        pl.semaphore_signal(barrier, inc=1, device_id=(r, other), device_id_type=MESH)

    live = lax.broadcasted_iota(I32, (1, entries), 1) < count_s[0]
    tile_row, slot_row = tile_v[...], slot_v[...]
    ray_row = jnp.concatenate([ray_v[...], jnp.zeros((1, 128 - n_region), I32)], axis=1)
    places = rows_v.shape[1]
    every = lax.broadcasted_iota(I32, ray_row.shape, 1) < n_region
    empty = lambda last, group, none: jnp.where(last < 0, none, last >> (group - 1))
    pad = lambda x: jnp.concatenate([x, jnp.zeros((1, places - x.shape[1]), I32)], axis=1)
    src, payload, opens, last = order(slot_row, live, tile_row, tiles, slots, 2, places)
    rows = [src, payload, opens, pad(empty(last, 2, pairs_f))]
    src, payload, opens, last = order(tile_row, live, slot_row, slots, tiles, 2, places)
    rows += [src, payload, opens, pad(empty(last, 2, pairs_b))]
    src, _, opens, last = order(ray_row, every, ray_row, 0, rays, 1, 128)
    rows += [pad(src), pad(opens), pad(empty(last, 1, n_region))]
    for i, row in enumerate(rows):
        rows_v[i : i + 1, :] = row
    to_scalar = pltpu.make_async_copy(rows_v, rows_s, sem_rows)
    to_scalar.start()

    load_v.wait()
    for t in range(tiles):
        vol_b[t] = vol[t].astype(BF)
    vol_b[tiles] = jnp.zeros((size, size), BF)
    for c, m in enumerate(sizes):
        recv2[c][slots] = jnp.zeros((m, size), BF)
    runs_f[pairs_f] = jnp.zeros((most, size), BF)
    runs_b[pairs_b] = jnp.zeros((most, size), F32)
    runs_p[n_region] = jnp.zeros((most, size), F32)
    to_scalar.wait()
    for load in load_b:
        load.wait()

    def products(left, base, transposed, runs, pairs, unroll, m):
        def step(g, total):
            for u in range(unroll):
                p = g * unroll + u
                e0, e1 = rows_s[base, 2 * p], rows_s[base, 2 * p + 1]
                k0, k1 = rows_s[base + 1, 2 * p], rows_s[base + 1, 2 * p + 1]
                opened = rows_s[base + 2, 2 * p]
                lhs = jnp.concatenate([left[k0], left[k1]], axis=1)
                rhs = jnp.concatenate([blocks[e0], blocks[e1]], axis=1 if transposed else 0)
                dims = (((1,), (1,)), ((), ())) if transposed else (((1,), (0,)), ((), ()))
                product = lax.dot_general(lhs, rhs, dims, preferred_element_type=F32)
                total = jnp.where(opened > 0, 0.0, total) + product
                runs[p, pl.ds(0, m), :] = total.astype(runs.dtype)
            return total

        lax.fori_loop(0, pairs // unroll, step, jnp.zeros((m, size), F32))

    def exchange(src, dst, ssem, rsem, c):
        for peer in peers:
            pltpu.make_async_remote_copy(
                src_ref=src.at[peer, parts[c]], dst_ref=dst[c].at[r],
                send_sem=ssem.at[c], recv_sem=rsem.at[c], device_id=(peer, a), device_id_type=MESH,
            ).start()
        dst[c][r] = src[r, parts[c], :]

    def arrived(dst, sem, c):
        part = dst[c].at[pl.ds(0, n_region - 1)]
        pltpu.make_async_copy(part, part, sem.at[c]).wait()

    for c, m in enumerate(sizes):
        rows_at = parts[c]
        products(vol_b.at[:, rows_at], 0, True, runs_f, pairs_f, UNROLL_F, m)
        for s in range(slots):
            send1[s, rows_at, :] = runs_f[rows_s[3, s], pl.ds(0, m), :]
        if c == 0:
            pl.semaphore_wait(barrier, len(peers) + len(others))
        exchange(send1, recv1, ssem1, rsem1, c)

    load_s.wait()
    for c, m in enumerate(sizes):
        rows_at = parts[c]
        arrived(recv1, rsem1, c)
        total = jnp.zeros((m, size), F32)
        for k in range(n_region):
            total = jnp.where(rows_s[9, k] > 0, 0.0, total) + recv1[c][rows_s[8, k]].astype(F32)
            runs_p[k, pl.ds(0, m), :] = total
        for j in range(rays):
            value = rw_v[j : j + 1, :] * (sino[j, rows_at, :] - runs_p[rows_s[10, j], pl.ds(0, m), :])
            res[j, rows_at, :] = value
            res_b[j, rows_at, :] = value.astype(BF)
        for s in range(n_region):
            send2[s, rows_at, :] = res_b[ray_s[s], rows_at, :]
        exchange(send2, recv2, ssem2, rsem2, c)

    for c, m in enumerate(sizes):
        rows_at = parts[c]
        arrived(recv2, rsem2, c)
        products(recv2[c], 4, False, runs_b, pairs_b, UNROLL_B, m)
        for t in range(tiles):
            value = runs_b[rows_s[7, t], pl.ds(0, m), :]
            grad[t, rows_at, :] = value
            send3[c][t // share, t % share] = value.astype(BF)
        for other in others:
            pltpu.make_async_remote_copy(
                src_ref=send3[c].at[other], dst_ref=recv3[c].at[a],
                send_sem=ssem3.at[c], recv_sem=rsem3.at[c], device_id=(r, other), device_id_type=MESH,
            ).start()
        recv3[c][a] = jnp.zeros((share, m, size), BF)

    for c, m in enumerate(sizes):
        rows_at = parts[c]
        part = recv3[c].at[pl.ds(0, n_angle - 1)]
        pltpu.make_async_copy(part, part, rsem3.at[c]).wait()
        for t in range(share):
            mine = a * share + t
            total = grad[mine, rows_at, :]
            for k in range(n_angle):
                total = total + recv3[c][k, t].astype(F32)
            upd[t, rows_at, :] = vol[mine, rows_at, :] + pw_v[pl.ds(mine, 1), :] * total

    for c in range(chunks):
        for src, sem in ((send1, ssem1), (send2, ssem2)):
            part = src.at[pl.ds(0, n_region - 1), parts[c]]
            pltpu.make_async_copy(part, part, sem.at[c]).wait()
        part = send3[c].at[pl.ds(0, n_angle - 1)]
        pltpu.make_async_copy(part, part, ssem3.at[c]).wait()


def store_kernel(upd, res, updated_h, residual_h, sem):
    copies = [
        pltpu.make_async_copy(res, residual_h, sem.at[0]),
        pltpu.make_async_copy(upd, updated_h, sem.at[1]),
    ]
    for copy in copies:
        copy.start()
    for copy in copies:
        copy.wait()


def up(value, step):
    return -(-value // step) * step


def body(volume, blocks, tile_of, slot_of, live_count, ray_of, sinogram, ray_weight, pixel_weight):
    n_region = lax.axis_size("region")
    n_angle = lax.axis_size("angle")
    entries, size, _ = blocks.shape
    tiles, rays = volume.shape[0], sinogram.shape[0]
    sizes = SIZES
    chunks, most = len(sizes), max(sizes)
    share = tiles // n_angle
    pairs_f = up((entries + n_region) // 2, UNROLL_F)
    pairs_b = up((entries + tiles) // 2, UNROLL_B)
    places = up(2 * max(pairs_f, pairs_b), 128)
    smem = pl.BlockSpec(memory_space=pltpu.SMEM)
    vmem = pl.BlockSpec(memory_space=pltpu.VMEM)
    hbm = pl.BlockSpec(memory_space=pl.ANY)
    upd, res = pl.pallas_call(
        functools.partial(kernel, n_region, n_angle, sizes),
        out_shape=(
            pltpu.VMEM((share, size, size), F32),
            pltpu.VMEM((rays, size, size), F32),
        ),
        in_specs=[smem, smem, vmem, vmem, vmem, vmem, vmem, hbm, hbm, hbm],
        out_specs=(vmem, vmem),
        scratch_shapes=[
            pltpu.VMEM((entries, size, size), BF),
            pltpu.VMEM((tiles, size, size), F32),
            pltpu.VMEM((rays, size, size), F32),
            pltpu.VMEM((tiles + 1, size, size), BF),
            pltpu.VMEM((pairs_f + 1, most, size), BF),
            pltpu.VMEM((pairs_b + 1, most, size), F32),
            pltpu.VMEM((n_region + 1, most, size), F32),
            pltpu.VMEM((16, places), I32),
            pltpu.SMEM((16, places), I32),
            pltpu.VMEM((n_region, size, size), BF),
            [pltpu.VMEM((n_region, m, size), BF) for m in sizes],
            pltpu.VMEM((rays, size, size), BF),
            pltpu.VMEM((n_region, size, size), BF),
            [pltpu.VMEM((n_region + 1, m, size), BF) for m in sizes],
            pltpu.VMEM((tiles, size, size), F32),
            [pltpu.VMEM((n_angle, share, m, size), BF) for m in sizes],
            [pltpu.VMEM((n_angle, share, m, size), BF) for m in sizes],
            pltpu.SemaphoreType.DMA((2 + LOADS,)),
            pltpu.SemaphoreType.DMA,
        ]
        + [pltpu.SemaphoreType.DMA((chunks,))] * 6,
        compiler_params=pltpu.CompilerParams(
            collective_id=0, has_side_effects=True, vmem_limit_bytes=56 * 2**20
        ),
    )(
        live_count, ray_of, tile_of.reshape(1, entries), slot_of.reshape(1, entries), ray_of.reshape(1, n_region),
        ray_weight, pixel_weight, volume, blocks, sinogram,
    )
    return pl.pallas_call(
        store_kernel,
        out_shape=(
            jax.ShapeDtypeStruct((share, size, size), F32),
            jax.ShapeDtypeStruct((rays, size, size), F32),
        ),
        in_specs=[vmem, vmem],
        out_specs=(hbm, hbm),
        scratch_shapes=[pltpu.SemaphoreType.DMA((2,))],
        compiler_params=pltpu.CompilerParams(vmem_limit_bytes=2**20),
    )(upd, res)


def solution(mesh):
    placed = (
        P("region", None, None),
        P(("region", "angle"), None, None),
        P(("region", "angle")),
        P(("region", "angle")),
        P(("region", "angle")),
        P(("region", "angle")),
        P(("region", "angle"), None, None),
        P(("region", "angle"), None),
        P("region", None),
    )
    return jax.shard_map(
        body,
        mesh=mesh,
        in_specs=placed,
        out_specs=(P(("region", "angle"), None, None), P(("region", "angle"), None, None)),
        check_vma=False,
    )
```

time: 81.1 us -> 73.2 us (0.903)
  local copies, waits for them, and re-layouts: 4.61 us -> 0 us
  Pallas kernels: 75 us -> 71.8 us
    unnamed x2 -> x0, local copies, waits for them, and re-layouts: 3.44 us -> none
    pallas_call x1 -> x2, Pallas kernels: 75 us -> 71.8 us  [the longest x1 70.9 us: body(): pl.pallas_call(functools.partial(kernel, n_region, n_angle, sizes), out_s...]
    reshape x1 -> x0, local copies, waits for them, and re-layouts: 1.17 us -> none  [body(): ray_row = jnp.pad(ray_of, (0, 128 - n_region)).reshape(1, 128)]
where the time goes in v2:
time: 73.2 us; the launch traced here: 73.1 us
  Pallas kernels  71.8 us (98%)
  between operations  1.29 us (2%)
    pallas_call x1, Pallas kernels, body(): pl.pallas_call(functools.partial(kernel, n_region, n_angle, sizes), out_s...  70.9 us

profile of v2, /device:TPU:1, one launch (start us, length us, event | category | flops | bytes accessed | tf_op | source)
XLA Modules:
  0.0 73.1 jit_solution(3964431734073003841)
XLA Ops:
  1.3 70.9 %shard_map.104 = (f32[2,128,128]{2,1,0:T(8,128)S(1)}, f32[8,128,128]{2,1,0:T(8,128)S(1)}) custom-call(s32[1]{0:T(128)S(6)} %copy.11.count_s, s32[32]{0:T(128)} %ray_s.1, s32[1,256]{1,0:T(1,128)} %bitcast.4, s32[1,256]{1,0:T(1,128)} %bitcast.5, s32[1,32]{1,0:T(1,128)} %bitcast.3, f32[8,128]{1,0:T(8,128)} %rw_v.1, f32[16,128]{1,0:T(8,128)} %pw_v.1, ...), custom_call_target="tpu_custom_call" | custom-call | tf_op jit(solution)/shard_map/pallas_call | solution.py:244
  72.2 0.8 %shard_map.105 = (f32[2,128,128]{2,1,0:T(8,128)}, f32[8,128,128]{2,1,0:T(8,128)}) custom-call(f32[2,128,128]{2,1,0:T(8,128)S(1)} %get-tuple-element.4.upd, f32[8,128,128]{2,1,0:T(8,128)S(1)} %get-tuple-element.5.res), custom_call_target="tpu_custom_call" | custom-call | tf_op jit(solution)/shard_map/pallas_call | solution.py:281

commit v3 on v2

--- a/solution.py
+++ b/solution.py
@@ -12,8 +12,8 @@
 F32 = jnp.float32
 I32 = jnp.int32
 
-SIZES = (48, 48, 32)
-UNROLL_F, UNROLL_B = 18, 17
+SIZES = (32, 32, 32, 32)
+UNROLL_F, UNROLL_B = 36, 34
 LOADS = 4
 NY = 4
 

time: 73.2 us -> 72 us (0.984)
  Pallas kernels: 71.8 us -> 70.6 us
    pallas_call x1, Pallas kernels: 70.9 us -> 69.7 us  [body(): pl.pallas_call(functools.partial(kernel, n_region, n_angle, sizes), out_s...]
where the time goes in v3:
time: 72 us; the launch traced here: 71.8 us
  Pallas kernels  70.6 us (98%)
  between operations  1.29 us (2%)
    pallas_call x1, Pallas kernels, body(): pl.pallas_call(functools.partial(kernel, n_region, n_angle, sizes), out_s...  69.7 us

profile of v3, /device:TPU:1, one launch (start us, length us, event | category | flops | bytes accessed | tf_op | source)
XLA Modules:
  0.0 71.8 jit_solution(11592117542232430004)
XLA Ops:
  1.3 69.7 %shard_map.104 = (f32[2,128,128]{2,1,0:T(8,128)S(1)}, f32[8,128,128]{2,1,0:T(8,128)S(1)}) custom-call(s32[1]{0:T(128)S(6)} %copy.11.count_s, s32[32]{0:T(128)} %ray_s.1, s32[1,256]{1,0:T(1,128)} %bitcast.4, s32[1,256]{1,0:T(1,128)} %bitcast.5, s32[1,32]{1,0:T(1,128)} %bitcast.3, f32[8,128]{1,0:T(8,128)} %rw_v.1, f32[16,128]{1,0:T(8,128)} %pw_v.1, ...), custom_call_target="tpu_custom_call" | custom-call | tf_op jit(solution)/shard_map/pallas_call | solution.py:244
  71.0 0.8 %shard_map.105 = (f32[2,128,128]{2,1,0:T(8,128)}, f32[8,128,128]{2,1,0:T(8,128)}) custom-call(f32[2,128,128]{2,1,0:T(8,128)S(1)} %get-tuple-element.4.upd, f32[8,128,128]{2,1,0:T(8,128)S(1)} %get-tuple-element.5.res), custom_call_target="tpu_custom_call" | custom-call | tf_op jit(solution)/shard_map/pallas_call | solution.py:281

commit v4 on v3

--- a/solution.py
+++ b/solution.py
@@ -178,6 +178,17 @@
             send2[s, rows_at, :] = res_b[ray_s[s], rows_at, :]
         exchange(send2, recv2, ssem2, rsem2, c)
 
+    def finish(c):
+        rows_at = parts[c]
+        part = recv3[c].at[pl.ds(0, n_angle - 1)]
+        pltpu.make_async_copy(part, part, rsem3.at[c]).wait()
+        for t in range(share):
+            mine = a * share + t
+            total = grad[mine, rows_at, :]
+            for k in range(n_angle):
+                total = total + recv3[c][k, t].astype(F32)
+            upd[t, rows_at, :] = vol[mine, rows_at, :] + pw_v[pl.ds(mine, 1), :] * total
+
     for c, m in enumerate(sizes):
         rows_at = parts[c]
         arrived(recv2, rsem2, c)
@@ -192,17 +203,9 @@
                 send_sem=ssem3.at[c], recv_sem=rsem3.at[c], device_id=(r, other), device_id_type=MESH,
             ).start()
         recv3[c][a] = jnp.zeros((share, m, size), BF)
-
-    for c, m in enumerate(sizes):
-        rows_at = parts[c]
-        part = recv3[c].at[pl.ds(0, n_angle - 1)]
-        pltpu.make_async_copy(part, part, rsem3.at[c]).wait()
-        for t in range(share):
-            mine = a * share + t
-            total = grad[mine, rows_at, :]
-            for k in range(n_angle):
-                total = total + recv3[c][k, t].astype(F32)
-            upd[t, rows_at, :] = vol[mine, rows_at, :] + pw_v[pl.ds(mine, 1), :] * total
+        if c:
+            finish(c - 1)
+    finish(chunks - 1)
 
     for c in range(chunks):
         for src, sem in ((send1, ssem1), (send2, ssem2)):
@@ -213,10 +216,10 @@
 
 
 def store_kernel(upd, res, updated_h, residual_h, sem):
-    copies = [
-        pltpu.make_async_copy(res, residual_h, sem.at[0]),
-        pltpu.make_async_copy(upd, updated_h, sem.at[1]),
-    ]
+    copies = [pltpu.make_async_copy(upd, updated_h, sem.at[0])]
+    for j in range(4):
+        part = pl.ds(2 * j, 2)
+        copies.append(pltpu.make_async_copy(res.at[part], residual_h.at[part], sem.at[1 + j]))
     for copy in copies:
         copy.start()
     for copy in copies:
@@ -286,7 +289,7 @@
         ),
         in_specs=[vmem, vmem],
         out_specs=(hbm, hbm),
-        scratch_shapes=[pltpu.SemaphoreType.DMA((2,))],
+        scratch_shapes=[pltpu.SemaphoreType.DMA((5,))],
         compiler_params=pltpu.CompilerParams(vmem_limit_bytes=2**20),
     )(upd, res)
 

time: 72 us -> 72 us (level)
  no operation moved by 1% of the time
where the time goes in v4:
time: 72 us; the launch traced here: 71.9 us
  Pallas kernels  70.6 us (98%)
  between operations  1.29 us (2%)
    pallas_call x1, Pallas kernels, body(): pl.pallas_call(functools.partial(kernel, n_region, n_angle, sizes), out_s...  69.7 us

profile of v4, /device:TPU:1, one launch (start us, length us, event | category | flops | bytes accessed | tf_op | source)
XLA Modules:
  0.0 71.9 jit_solution(13087905680051661288)
XLA Ops:
  1.3 69.7 %shard_map.104 = (f32[2,128,128]{2,1,0:T(8,128)S(1)}, f32[8,128,128]{2,1,0:T(8,128)S(1)}) custom-call(s32[1]{0:T(128)S(6)} %copy.11.count_s, s32[32]{0:T(128)} %ray_s.1, s32[1,256]{1,0:T(1,128)} %bitcast.4, s32[1,256]{1,0:T(1,128)} %bitcast.5, s32[1,32]{1,0:T(1,128)} %bitcast.3, f32[8,128]{1,0:T(8,128)} %rw_v.1, f32[16,128]{1,0:T(8,128)} %pw_v.1, ...), custom_call_target="tpu_custom_call" | custom-call | tf_op jit(solution)/shard_map/pallas_call | solution.py:247
  71.0 0.9 %shard_map.105 = (f32[2,128,128]{2,1,0:T(8,128)}, f32[8,128,128]{2,1,0:T(8,128)}) custom-call(f32[2,128,128]{2,1,0:T(8,128)S(1)} %get-tuple-element.4.upd, f32[8,128,128]{2,1,0:T(8,128)S(1)} %get-tuple-element.5.res), custom_call_target="tpu_custom_call" | custom-call | tf_op jit(solution)/shard_map/pallas_call | solution.py:284
